TPU v7x, 32 devices: a whole 2x2x4 slice. The times are simulated.
32 devices in a mesh: tok: 16 (over z, y, core), tp: 2 (over x).
Axes of the slice: x: 2, y: 2, z: 4, core: 2. Of those that a mesh axis runs over, the one named last changes fastest.
Arguments:
- hidden_in: bfloat16 [4096, 4096], P('tok', 'tp'), may hold values from -6 to 6
- norm_gain: float32 [4096], replicated, may hold values from 0.5 to 9, as said below
- w_query: bfloat16 [4096, 4096], P(None, 'tp'), may hold values from -0.09375 to 0.09375
- w_key: bfloat16 [4096, 1024], P(None, 'tp'), may hold values from -0.09375 to 0.09375
- w_value: bfloat16 [4096, 1024], P(None, 'tp'), may hold values from -0.09375 to 0.09375
- w_out: bfloat16 [4096, 4096], P('tp'), may hold values from -0.5 to 0.5
- doc_ids: int32 [4096], replicated, may hold values from 0 to 3, never falling along the last dimension, each value on 1 to 3072 neighbouring positions
Outputs:
- hidden_out: bfloat16 [4096, 4096], P('tok', 'tp')
- joint_cov: float32 [2, 4096, 2, 4096], P(None, 'tok', None, 'tp')
Inputs may be any that keep to these rules, and one draw needn't show every extreme that they name: `norm_gain`: each channel's gain is positive. `doc_ids`: document numbers never fall along the tokens; a document holds 1 to 3072 tokens.
All inputs are finite; a program needn't handle non-finite values.
Results may differ from a plain program's by a relative error of at most 0.013.
The roundings to bfloat16 on the way count: a program that leaves them out, or rounds other values in their place, can miss the bound.
Values may be sent and summed in bfloat16 or wider, within the bound.
A program may use at most 192 MiB of HBM per device.

v0:
```python
import jax
import jax.numpy as jnp
from jax import lax
from jax.sharding import PartitionSpec as P

HS = 128
epsilon = 1e-05
rope_base = 500000.0


def broadcast(block, axis, source):
    block = jnp.where(lax.axis_index(axis) == source, block, jnp.zeros_like(block))
    return lax.psum(block, axis)


def rotate(vectors, positions):
    half_dim = vectors.shape[-1] // 2
    inv_freq = rope_base ** (-(jnp.arange(half_dim, dtype=jnp.float32) * 2.0) / vectors.shape[-1])
    angles = positions.astype(jnp.float32)[:, None] * inv_freq[None, :]
    cosine = jnp.cos(angles)[:, None, :]
    sine_part = jnp.sin(angles)[:, None, :]
    first_half = vectors[..., :half_dim]
    second_half = vectors[..., half_dim:]
    return jnp.concatenate(
        [
            first_half * cosine - second_half * sine_part,
            second_half * cosine + first_half * sine_part,
        ],
        axis=-1,
    )


def on_device(hidden_in, norm_gain, w_query, w_key, w_value, w_out, doc_ids):
    tok_rows = hidden_in.shape[0]
    col_width = hidden_in.shape[1]
    tok_count = lax.axis_size("tok")
    tok_index = lax.axis_index("tok")
    all_rows = tok_rows * tok_count
    full_in = lax.all_gather(hidden_in, "tp", axis=1, tiled=True)
    model_width = full_in.shape[1]
    row_width = model_width // tok_count
    widened = full_in.astype(jnp.float32)
    factor = lax.rsqrt(jnp.mean(widened * widened, axis=1, keepdims=True) + epsilon)
    normed = (widened * factor * norm_gain[None, :]).astype(jnp.bfloat16)
    kv_heads = w_key.shape[1] // HS
    groups = w_query.shape[1] // w_key.shape[1]
    first_row = tok_index * tok_rows
    positions = first_row + jnp.arange(tok_rows, dtype=jnp.int32)
    key_local = rotate(
        jnp.dot(normed, w_key, preferred_element_type=jnp.float32).reshape(tok_rows, kv_heads, HS),
        positions % all_rows,
    )
    key_local = key_local.astype(jnp.bfloat16).reshape(tok_rows, kv_heads * HS)
    value_local = jnp.dot(normed, w_value, preferred_element_type=jnp.float32).astype(jnp.bfloat16)
    key_rows, value_rows = (
        lax.all_gather(key_local, "tok", axis=0, tiled=True),
        lax.all_gather(value_local, "tok", axis=0, tiled=True),
    )
    queries = rotate(
        jnp.dot(normed, w_query, preferred_element_type=jnp.float32).reshape(
            tok_rows, kv_heads * groups, HS
        ),
        positions % all_rows,
    )
    queries = queries.astype(jnp.bfloat16).reshape(tok_rows, kv_heads, groups, HS)
    key_seq = key_rows.reshape(all_rows, kv_heads, HS)
    value_seq = value_rows.reshape(all_rows, kv_heads, HS)
    key_pos = jnp.arange(all_rows, dtype=jnp.int32)
    query_doc = lax.dynamic_slice_in_dim(doc_ids, first_row, tok_rows, 0)
    allowed = (query_doc[:, None] == doc_ids[None, :]) & (key_pos[None, :] <= positions[:, None])
    scores = jnp.einsum(
        "qhgd,khd->hgqk", queries, key_seq, preferred_element_type=jnp.float32
    ) * HS ** (-0.5)
    scores = jnp.where(allowed[None, None], scores, -jnp.inf)
    row_max = jnp.max(scores, axis=-1, keepdims=True)
    weights = jnp.exp(scores - row_max)
    weight_sum = jnp.sum(weights, axis=-1, keepdims=True)
    blended = (
        jnp.einsum(
            "hgqk,khd->hgqd",
            weights.astype(jnp.bfloat16),
            value_seq,
            preferred_element_type=jnp.float32,
        )
        / weight_sum
    )
    attended = (
        jnp.transpose(blended, (2, 0, 1, 3))
        .astype(jnp.bfloat16)
        .reshape(tok_rows, kv_heads * groups * HS)
    )
    partial_out = jnp.dot(attended, w_out, preferred_element_type=jnp.float32)
    summed = lax.psum_scatter(partial_out, "tp", scatter_dimension=1, tiled=True)
    hidden_out = (hidden_in.astype(jnp.float32) + summed).astype(jnp.bfloat16)
    columns = lax.all_gather(jnp.stack([hidden_in, hidden_out], axis=1), "tok", axis=0, tiled=True)
    offset = tok_index * row_width % col_width
    owner_rank = tok_index * row_width // col_width
    own_rows = lax.dynamic_slice_in_dim(columns, offset, row_width, 2)
    row_block = broadcast(own_rows, "tp", owner_rank).reshape(all_rows, 2 * row_width)
    flat_cols = columns.reshape(all_rows, 2 * col_width)
    gram_block = lax.dot_general(
        row_block, flat_cols, (((0,), (0,)), ((), ())), preferred_element_type=jnp.float32
    )
    col_sum = jnp.sum(flat_cols, axis=0, dtype=jnp.float32)
    row_mean = jnp.sum(row_block, axis=0, dtype=jnp.float32) / all_rows
    col_mean = col_sum / all_rows
    joint_cov = (gram_block / all_rows - row_mean[:, None] * col_mean[None, :]).reshape(
        2, row_width, 2, col_width
    )
    return (hidden_out, joint_cov)


def solution(mesh):
    return jax.shard_map(
        on_device,
        mesh=mesh,
        in_specs=(
            P("tok", "tp"),
            P(),
            P(None, "tp"),
            P(None, "tp"),
            P(None, "tp"),
            P("tp", None),
            P(),
        ),
        out_specs=(P("tok", "tp"), P(None, "tok", None, "tp")),
        check_vma=False,
    )
```

profile of v0, /device:TPU:0, one launch (start us, length us, event | category | flops | bytes accessed | tf_op | source)
XLA Modules:
  0.0 588.9 jit_solution(13531846354874264925)
XLA Ops:
  7.2 0.0 all-gather.5.cloned.1.call-start
  7.2 0.7 all-gather.5.cloned.1.call-update
  7.9 0.0 all-gather.7.cloned.1.call-start
  8.0 0.5 multiply_cosine_fusion
  8.5 36.8 %all-gather.5.cloned.1.call-done = bf16[256,4096]{1,0:T(8,128)(2,1)} async-done(((bf16[256,2048]{1,0:T(8,128)(2,1)}), bf16[256,4096]{1,0:T(8,128)(2,1)}) %all-gather.5.cloned.1.call-update) | async-done | bytes 2097168 | tf_op jit(solution)/shard_map/all_gather | solution.py:39
  45.4 2.1 fusion.6
  47.5 4.1 fusion.24
  51.6 0.0 copy-start.5
  51.6 0.2 reshape.184
  51.8 0.5 subtract_convert_fusion.1
  52.3 0.4 pad_maximum_fusion.1
  52.7 0.9 copy.13
  53.5 0.0 all-gather.7.cloned.1.call-update
  53.6 0.0 all-gather.9.cloned.1.call-start
  53.6 0.1 dynamic_slice.6
  53.7 1.9 fusion.9
  55.6 8.3 %convolution_bitcast_fusion = f32[32,8,16,128]{3,1,2,0:T(8,128)S(1)} fusion(bf16[4096,2048]{1,0:T(8,128)(2,1)} %param.9, bf16[256,4096]{1,0:T(8,128)(2,1)S(1)} %copy-done.2, f32[4096]{0:T(1024)S(1)} %copy-done.5, f32[256]{0:T(256)S(1)} %add_rsqrt_fusion), kind=kOutput, calls=%fused_computation.24 | convolution fusion | flops 4299161600 | bytes 20988928 | tf_op jit(solution)/shard_map/dot_general | solution.py:60
  63.9 0.4 copy.27
  64.3 0.8 subtract_convert_fusion
  65.1 1.2 copy.14
  66.3 1.2 copy.15
  67.5 2.0 convolution_convert_fusion
  69.5 0.0 all-gather.9.cloned.1.call-update
  69.6 0.2 reduce-scatter.2.cloned.1.call-start
  69.8 36.4 %all-gather.7.cloned.1.call-done = bf16[4096,512]{0,1:T(8,128)(2,1)} async-done(((bf16[256,512]{0,1:T(8,128)(2,1)}), bf16[4096,512]{0,1:T(8,128)(2,1)}) %all-gather.7.cloned.1.call-update) | async-done | bytes 4194320 | tf_op jit(solution)/shard_map/all_gather | solution.py:56
  106.2 28.9 %fusion.2 = (f32[4,4,256]{2,1,0:T(4,128)S(1)}, f32[4,4096,256,4]{2,1,3,0:T(8,128)}) fusion(pred[256,4096]{0,1:T(8,128)(4,1)S(1)} %fusion.9, bf16[4096,4,128,1]{0,2,3,1:T(8,128)(2,1)} %bitcast.65, bf16[256,4,4,64]{3,0,2,1:T(8,128)(2,1)} %bitcast.60, bf16[256,4,4,64]{3,0,2,1:T(8,128)(2,1)} %bitcast.59), kind=kOutput, calls=%fused_computation.5 | convolution fusion | flops 4347392000 | bytes 73416704 | tf_op jit(solution)/shard_map/qhgd,khd->hgqk/dot_general | solution.py:71
  135.2 22.1 %fusion = f32[4,4,256]{2,1,0:T(4,128)S(1)} fusion(f32[4,4096,256,4]{2,1,3,0:T(8,128)} %get-tuple-element.9, f32[4,4,256]{2,1,0:T(4,128)S(1)} %get-tuple-element.8, pred[256,4096]{0,1:T(8,128)(4,1)S(1)} %fusion.9), kind=kLoop, calls=%fused_computation.3 | loop fusion | flops 67104768 | bytes 68190208 | tf_op jit(solution)/shard_map/reduce_sum | solution.py:77
  157.3 0.0 all-gather.9.cloned.1.call-done
  157.3 6.3 %copy.26 = bf16[4096,512]{0,1:T(8,128)(2,1)} copy(bf16[4096,512]{1,0:T(8,128)(2,1)} %all-gather.9.cloned.1.call-done) | data formatting | bytes 8388608 | tf_op jit(solution)/shard_map/reshape | solution.py:67
  163.6 25.5 %fusion.10 = bf16[256,4,4,128]{0,3,2,1:T(8,128)(2,1)S(1)} fusion(bf16[4096,4,128,1]{0,2,3,1:T(8,128)(2,1)} %bitcast.55, f32[4,4096,256,4]{2,1,3,0:T(8,128)} %get-tuple-element.9, f32[4,4,256]{2,1,0:T(4,128)S(1)} %get-tuple-element.8, pred[256,4096]{0,1:T(8,128)(4,1)S(1)} %fusion.9, f32[256,4,4]{0,2,1:T(4,128)S(1)} %bitcast.63), kind=kOutput, calls=%fused_computation.20 | convolution fusion | flops 4363124736 | bytes 73433088 | tf_op jit(solution)/shard_map/hgqk,khd->hgqd/dot_general | solution.py:79
  189.2 10.4 %fusion.26 = f32[256,4096]{1,0:T(8,128)} fusion(bf16[256,2048]{0,1:T(8,128)(2,1)S(1)} %bitcast.58, bf16[2048,4096]{1,0:T(8,128)(2,1)} %param.12), kind=kOutput, calls=%fused_computation.49 | convolution fusion | flops 4294967296 | bytes 22020096 | tf_op jit(solution)/shard_map/dot_general | solution.py:92
  199.6 0.0 reduce-scatter.2.cloned.1.call-update
  199.6 0.0 all-gather.11.cloned.1.call-start
  199.7 52.7 %reduce-scatter.2.cloned.1.call-done = f32[256,2048]{1,0:T(8,128)} async-done(((f32[256,4096]{1,0:T(8,128)}), f32[256,2048]{1,0:T(8,128)}) %reduce-scatter.2.cloned.1.call-update) | async-done | bytes 2097168 | tf_op jit(solution)/shard_map/reduce_scatter | solution.py:93
  252.4 1.9 add_convert_fusion
  254.3 1.7 pad_maximum_fusion
  256.0 0.0 all-gather.11.cloned.1.call-update
  256.0 0.0 all-reduce.2.cloned.1.call-start
  256.1 168.1 %all-gather.11.cloned.1.call-done = bf16[4096,2,2048]{2,0,1:T(8,128)(2,1)} async-done(((bf16[256,2,2048]{2,0,1:T(8,128)(2,1)}), bf16[4096,2,2048]{2,0,1:T(8,128)(2,1)}) %all-gather.11.cloned.1.call-update) | async-done | bytes 33554448 | tf_op jit(solution)/shard_map/all_gather | solution.py:95
  424.2 4.9 dynamic-slice_select_fusion
  429.1 0.0 all-reduce.2.cloned.1.call-update
  429.2 12.4 %convert_reduce_fusion = f32[2,2048]{1,0:T(2,128)S(1)} fusion(bf16[4096,2,2048]{2,0,1:T(8,128)(2,1)} %all-gather.11.cloned.1.call-done), kind=kLoop, calls=%fused_computation.1 | loop fusion | flops 33550336 | bytes 33570816 | tf_op jit(solution)/shard_map/reduce_sum | solution.py:104
  441.6 40.5 %copy.20 = bf16[4096,2,2048]{0,2,1:T(8,128)(2,1)} copy(bf16[4096,2,2048]{2,0,1:T(8,128)(2,1)} %all-gather.11.cloned.1.call-done) | data formatting | bytes 67108864 | tf_op jit(solution)/shard_map/all_gather | solution.py:95
  482.0 55.2 %all-reduce.2.cloned.1.call-done = bf16[4096,2,256]{2,0,1:T(8,128)(2,1)} async-done(((bf16[4096,2,256]{2,0,1:T(8,128)(2,1)}), bf16[4096,2,256]{2,0,1:T(8,128)(2,1)}) %all-reduce.2.cloned.1.call-update) | async-done | bytes 4194320 | tf_op jit(solution)/shard_map/psum | solution.py:13
  537.2 2.8 convert_reduce_fusion.1
  540.0 6.3 %copy.19 = bf16[4096,2,256]{0,2,1:T(8,128)(2,1)} copy(bf16[4096,2,256]{2,0,1:T(8,128)(2,1)} %all-reduce.2.cloned.1.call-done) | data formatting | bytes 8388608 | tf_op jit(solution)/shard_map/psum | solution.py:13
  546.3 24.0 %multiply_subtract_fusion = f32[512,4096]{1,0:T(8,128)} fusion(bf16[4096,512]{0,1:T(8,128)(2,1)} %bitcast.56, bf16[4096,4096]{0,1:T(8,128)(2,1)} %bitcast.52, f32[4096]{0:T(1024)S(1)} %bitcast.62, f32[512]{0:T(512)S(1)} %bitcast.64), kind=kOutput, calls=%fused_computation.8 | convolution fusion | flops 17186160640 | bytes 46155776 | tf_op jit(solution)/shard_map/dot_general | solution.py:101
  570.4 11.7 %reshape.191 = f32[2,256,2,2048]{3,2,1,0:T(2,128)} reshape(f32[512,4096]{1,0:T(8,128)} %multiply_subtract_fusion) | data formatting | bytes 16777216 | tf_op jit(solution)/shard_map/reshape | solution.py:107
  (19 shorter events, 0.1 us)
Async XLA Ops:
  7.2 38.2 %all-gather.5.cloned.1.call-start = ((), (), s32[]{:S(2)}) async-start(), calls=%async_computation.1 | async-start | bytes 3145728 | tf_op jit(solution)/shard_map/all_gather | solution.py:39
  7.9 98.3 %all-gather.7.cloned.1.call-start = ((), (), s32[]{:S(2)}) async-start(), calls=%async_computation.2 | async-start | bytes 4456448 | tf_op jit(solution)/shard_map/all_gather | solution.py:56
  51.6 2.0 copy-start.3
  51.6 4.0 copy-start.2
  51.6 4.0 copy-start.5
  53.6 103.7 %all-gather.9.cloned.1.call-start = ((), (), s32[]{:S(2)}) async-start(), calls=%async_computation.3 | async-start | bytes 4456448 | tf_op jit(solution)/shard_map/all_gather | solution.py:57
  64.3 3.3 copy-start.4
  69.6 182.8 %reduce-scatter.2.cloned.1.call-start = ((), (), s32[]{:S(2)}) async-start(), calls=%async_computation.4 | async-start | bytes 6291456 | tf_op jit(solution)/shard_map/reduce_scatter | solution.py:93
  199.6 52.8 %copy-start = (bf16[256,2048]{1,0:T(8,128)(2,1)S(1)}, bf16[256,2048]{1,0:T(8,128)(2,1)}, u32[]{:S(2)}) copy-start(bf16[256,2048]{1,0:T(8,128)(2,1)} %param.7) | copy-start | bytes 3145732
  199.6 224.6 %all-gather.11.cloned.1.call-start = ((), (), s32[]{:S(2)}) async-start(), calls=%async_computation.5 | async-start | bytes 35651584 | tf_op jit(solution)/shard_map/all_gather | solution.py:95
  254.3 174.8 %copy-start.1 = (bf16[256,2048]{1,0:T(8,128)(2,1)}, bf16[256,2048]{1,0:T(8,128)(2,1)S(1)}, u32[]{:S(2)}) copy-start(bf16[256,2048]{1,0:T(8,128)(2,1)S(1)} %add_convert_fusion) | copy-start | bytes 3145732
  256.0 281.2 %all-reduce.2.cloned.1.call-start = ((), (), s32[]{:S(2)}) async-start(), calls=%async_computation.6 | async-start | bytes 8388608 | tf_op jit(solution)/shard_map/psum | solution.py:13
Sparse Core Ops, SparseCore 0:
  9.5 35.8 all-gather.4
  53.7 52.4 all-gather.6
  108.4 48.5 all-gather.8
  199.7 52.6 reduce-scatter.1
  256.1 168.0 all-gather.10
  429.3 107.8 all-reduce.1
where the time goes:
time: 591 us; the launch traced here: 589 us
  waiting for transfers between devices  350 us (59%)
  matrix products  103 us (17%)
  local copies, waits for them, and re-layouts  68.9 us (12%)
  other arithmetic  51.8 us (9%)
  between operations  14.4 us (2%)
    all_gather x1, waiting for transfers between devices, on_device(): lax.all_gather(jnp.stack([hidden_in, hidden_out], axis=1), 'tok', axis=0,...  168 us
    psum x1, waiting for transfers between devices, broadcast(): return lax.psum(block, axis)  55.2 us
    reduce_scatter x1, waiting for transfers between devices, on_device(): lax.psum_scatter(partial_out, 'tp', scatter_dimension=1, tiled=True)  52.7 us
    all_gather x1, local copies, waits for them, and re-layouts, on_device(): lax.all_gather(jnp.stack([hidden_in, hidden_out], axis=1), 'tok', axis=0,...  40.5 us
    all_gather x1, waiting for transfers between devices, on_device(): full_in = lax.all_gather(hidden_in, 'tp', axis=1, tiled=True)  36.8 us
    all_gather x1, waiting for transfers between devices, on_device(): lax.all_gather(key_local, 'tok', axis=0, tiled=True)  36.4 us
    dot_general x1, matrix products, on_device(): jnp.einsum('qhgd,khd->hgqk', queries, key_seq, preferred_element_type=jnp...  28.9 us
    dot_general x1, matrix products, on_device(): jnp.einsum('hgqk,khd->hgqd', weights.astype(jnp.bfloat16), value_seq, pre...  25.5 us
  transfers between devices with their start and end apart: 6, of which 5 were waited for; matrix products, arithmetic and copies ran while one was open for 20% of the time, Pallas kernels for 0%

commit v1 on v0

--- a/solution.py
+++ b/solution.py
@@ -36,7 +36,7 @@
     tok_count = lax.axis_size("tok")
     tok_index = lax.axis_index("tok")
     all_rows = tok_rows * tok_count
-    full_in = lax.all_gather(hidden_in, "tp", axis=1, tiled=True)
+    full_in = jnp.concatenate(lax.all_gather(hidden_in, "tp"), axis=1)
     model_width = full_in.shape[1]
     row_width = model_width // tok_count
     widened = full_in.astype(jnp.float32)

time: 591 us -> 596 us (level)
  waiting for transfers between devices: 350 us -> 308 us
  local copies, waits for them, and re-layouts: 68.9 us -> 107 us
  other arithmetic: 51.8 us -> 61.2 us
    all_gather x1, waiting for transfers between devices: 36.4 us -> 0.02 us  [on_device(): lax.all_gather(key_local, 'tok', axis=0, tiled=True)]
    dot_general x0 -> x2, local copies, waits for them, and re-layouts: none -> 27.3 us  [the longest x1 20.9 us: on_device(): jnp.dot(normed, w_query, preferred_element_type=jnp.float32)]
    all_gather x1, waiting for transfers between devices: 36.8 us -> 30 us  [on_device(): full_in = jnp.concatenate(lax.all_gather(hidden_in, 'tp'), axis=1)]
  transfers between devices with their start and end apart: 6 -> 6, of which waited for: 5 -> 5; matrix products, arithmetic and copies ran while one was open for 20% -> 27% of each run, Pallas kernels for 0% -> 0%
where the time goes in v1:
time: 596 us; the launch traced here: 593 us
  waiting for transfers between devices  308 us (52%)
  local copies, waits for them, and re-layouts  107 us (18%)
  matrix products  103 us (17%)
  other arithmetic  61.2 us (10%)
  between operations  14.3 us (2%)
    all_gather x1, waiting for transfers between devices, on_device(): lax.all_gather(jnp.stack([hidden_in, hidden_out], axis=1), 'tok', axis=0,...  168 us
    psum x1, waiting for transfers between devices, broadcast(): return lax.psum(block, axis)  54.6 us
    reduce_scatter x1, waiting for transfers between devices, on_device(): lax.psum_scatter(partial_out, 'tp', scatter_dimension=1, tiled=True)  53.2 us
    all_gather x1, local copies, waits for them, and re-layouts, on_device(): lax.all_gather(jnp.stack([hidden_in, hidden_out], axis=1), 'tok', axis=0,...  41 us
    all_gather x1, waiting for transfers between devices, on_device(): full_in = jnp.concatenate(lax.all_gather(hidden_in, 'tp'), axis=1)  30 us
    dot_general x1, matrix products, on_device(): jnp.einsum('qhgd,khd->hgqk', queries, key_seq, preferred_element_type=jnp...  26.8 us
    dot_general x1, matrix products, on_device(): jnp.einsum('hgqk,khd->hgqd', weights.astype(jnp.bfloat16), value_seq, pre...  25.5 us
    dot_general x1, matrix products, on_device(): lax.dot_general(row_block, flat_cols, (((0,), (0,)), ((), ())), preferred...  24.1 us
  transfers between devices with their start and end apart: 6, of which 5 were waited for; matrix products, arithmetic and copies ran while one was open for 27% of the time, Pallas kernels for 0%

profile of v1, /device:TPU:0, one launch (start us, length us, event | category | flops | bytes accessed | tf_op | source)
XLA Modules:
  0.0 593.4 jit_solution(17636859583533429064)
XLA Ops:
  7.2 0.0 all-gather.12.cloned.1.call-start
  7.2 0.7 all-gather.12.cloned.1.call-update
  7.9 0.0 all-gather.6.cloned.1.call-start
  7.9 0.7 mul.161
  8.7 6.3 %copy.56 = bf16[512,4096]{1,0:T(8,128)(2,1)} copy(bf16[512,4096]{0,1:T(8,128)(2,1)} %bitcast.79) | data formatting | bytes 8388608 | tf_op jit(solution)/shard_map/dot_general | solution.py:50
  15.0 0.3 multiply_cosine_fusion
  15.4 30.0 %all-gather.12.cloned.1.call-done = bf16[512,2048]{1,0:T(8,128)(2,1)} async-done(((bf16[256,2048]{1,0:T(8,128)(2,1)}), bf16[512,2048]{1,0:T(8,128)(2,1)}) %all-gather.12.cloned.1.call-update) | async-done | bytes 2097168 | tf_op jit(solution)/shard_map/all_gather | solution.py:39
  45.4 2.1 fusion.6
  47.5 2.2 fusion.12
  49.7 2.5 copy.37
  52.3 4.1 fusion.25
  56.3 0.1 subtract_convert_fusion.1
  56.4 0.7 pad_maximum_fusion.1
  57.2 0.0 all-gather.8.cloned.1.call-start
  57.2 20.9 %copy.60 = bf16[2048,4096]{1,0:T(8,128)(2,1)} copy(bf16[2048,4096]{0,1:T(8,128)(2,1)} %bitcast.76) | data formatting | bytes 33554432 | tf_op jit(solution)/shard_map/dot_general | solution.py:60
  78.2 0.1 dynamic_slice.6
  78.2 1.9 fusion.11
  80.1 9.8 %fusion.26 = f32[256,16,128]{0,2,1:T(8,128)} fusion(bf16[256,4096,1]{0,1,2:T(8,128)(2,1)S(1)} %bitcast.87, bf16[16,128,4096]{2,1,0:T(8,128)(2,1)} %bitcast.77), kind=kOutput, calls=%fused_computation.53 | convolution fusion | flops 4294967296 | bytes 20971520 | tf_op jit(solution)/shard_map/dot_general | solution.py:60
  89.9 3.0 subtract_convert_fusion
  92.9 2.3 copy.42
  95.3 2.4 copy.43
  97.6 2.5 convert_bitcast_fusion
  100.2 5.4 copy.45
  105.5 2.7 fusion.10
  108.3 0.9 copy-done.8
  109.2 2.0 convolution_convert_fusion
  111.2 0.2 reduce-scatter.2.cloned.1.call-start
  111.4 0.0 all-gather.6.cloned.1.call-done
  111.5 26.8 %fusion.2 = (f32[4,4,256]{2,1,0:T(4,128)S(1)}, f32[4,4096,256,4]{2,1,3,0:T(8,128)}) fusion(pred[256,4096]{0,1:T(8,128)(4,1)S(1)} %fusion.11, bf16[4096,4,128,1]{0,2,3,1:T(8,128)(2,1)} %bitcast.93, bf16[256,4,4,64]{3,0,2,1:T(8,128)(2,1)S(1)} %copy-done.5, bf16[256,4,4,64]{3,0,2,1:T(8,128)(2,1)S(1)} %copy-done.4), kind=kOutput, calls=%fused_computation.5 | convolution fusion | flops 4347392000 | bytes 73416704 | tf_op jit(solution)/shard_map/qhgd,khd->hgqk/dot_general | solution.py:71
  138.3 22.0 %fusion = f32[4,4,256]{2,1,0:T(4,128)S(1)} fusion(f32[4,4096,256,4]{2,1,3,0:T(8,128)} %get-tuple-element.9, f32[4,4,256]{2,1,0:T(4,128)S(1)} %get-tuple-element.8, pred[256,4096]{0,1:T(8,128)(4,1)S(1)} %fusion.11), kind=kLoop, calls=%fused_computation.3 | loop fusion | flops 67104768 | bytes 68190208 | tf_op jit(solution)/shard_map/reduce_sum | solution.py:77
  160.3 1.2 all-gather.8.cloned.1.call-done
  161.5 6.3 %copy.61 = bf16[4096,512]{0,1:T(8,128)(2,1)} copy(bf16[4096,512]{1,0:T(8,128)(2,1)} %all-gather.8.cloned.1.call-done) | data formatting | bytes 8388608 | tf_op jit(solution)/shard_map/reshape | solution.py:67
  167.8 25.5 %fusion.13 = bf16[256,4,4,128]{0,3,2,1:T(8,128)(2,1)S(1)} fusion(bf16[4096,4,128,1]{0,2,3,1:T(8,128)(2,1)} %bitcast.81, f32[4,4096,256,4]{2,1,3,0:T(8,128)} %get-tuple-element.9, f32[4,4,256]{2,1,0:T(4,128)S(1)} %get-tuple-element.8, pred[256,4096]{0,1:T(8,128)(4,1)S(1)} %fusion.11, f32[256,4,4]{0,2,1:T(4,128)S(1)} %bitcast.91), kind=kOutput, calls=%fused_computation.25 | convolution fusion | flops 4363124736 | bytes 73433088 | tf_op jit(solution)/shard_map/hgqk,khd->hgqd/dot_general | solution.py:79
  193.3 10.2 %fusion.27 = f32[256,4096]{1,0:T(8,128)} fusion(bf16[256,2048]{0,1:T(8,128)(2,1)S(1)} %bitcast.88, bf16[2048,4096]{1,0:T(8,128)(2,1)} %param.12), kind=kOutput, calls=%fused_computation.54 | convolution fusion | flops 4294967296 | bytes 22020096 | tf_op jit(solution)/shard_map/dot_general | solution.py:92
  203.5 0.0 all-gather.10.cloned.1.call-start
  203.6 53.2 %reduce-scatter.2.cloned.1.call-done = f32[256,2048]{1,0:T(8,128)} async-done(((f32[256,4096]{1,0:T(8,128)}), f32[256,2048]{1,0:T(8,128)}) %reduce-scatter.2.cloned.1.call-update) | async-done | bytes 2097168 | tf_op jit(solution)/shard_map/reduce_scatter | solution.py:93
  256.8 1.9 add_convert_fusion
  258.7 1.7 pad_maximum_fusion
  260.4 0.3 all-reduce.2.cloned.1.call-start
  260.7 167.9 %all-gather.10.cloned.1.call-done = bf16[4096,2,2048]{2,0,1:T(8,128)(2,1)} async-done(((bf16[256,2,2048]{2,0,1:T(8,128)(2,1)}), bf16[4096,2,2048]{2,0,1:T(8,128)(2,1)}) %all-gather.10.cloned.1.call-update) | async-done | bytes 33554448 | tf_op jit(solution)/shard_map/all_gather | solution.py:95
  428.6 4.9 dynamic-slice_select_fusion
  433.5 12.4 %convert_reduce_fusion = f32[2,2048]{1,0:T(2,128)S(1)} fusion(bf16[4096,2,2048]{2,0,1:T(8,128)(2,1)} %all-gather.10.cloned.1.call-done), kind=kLoop, calls=%fused_computation.1 | loop fusion | flops 33550336 | bytes 33570816 | tf_op jit(solution)/shard_map/reduce_sum | solution.py:104
  445.9 41.0 %copy.49 = bf16[4096,2,2048]{0,2,1:T(8,128)(2,1)} copy(bf16[4096,2,2048]{2,0,1:T(8,128)(2,1)} %all-gather.10.cloned.1.call-done) | data formatting | bytes 67108864 | tf_op jit(solution)/shard_map/all_gather | solution.py:95
  487.0 54.6 %all-reduce.2.cloned.1.call-done = bf16[4096,2,256]{2,0,1:T(8,128)(2,1)} async-done(((bf16[4096,2,256]{2,0,1:T(8,128)(2,1)}), bf16[4096,2,256]{2,0,1:T(8,128)(2,1)}) %all-reduce.2.cloned.1.call-update) | async-done | bytes 4194320 | tf_op jit(solution)/shard_map/psum | solution.py:13
  541.6 2.8 convert_reduce_fusion.1
  544.4 6.3 %copy.48 = bf16[4096,2,256]{0,2,1:T(8,128)(2,1)} copy(bf16[4096,2,256]{2,0,1:T(8,128)(2,1)} %all-reduce.2.cloned.1.call-done) | data formatting | bytes 8388608 | tf_op jit(solution)/shard_map/psum | solution.py:13
  550.7 24.1 %multiply_subtract_fusion = f32[512,4096]{1,0:T(8,128)} fusion(bf16[4096,512]{0,1:T(8,128)(2,1)} %bitcast.82, bf16[4096,4096]{0,1:T(8,128)(2,1)} %bitcast.74, f32[4096]{0:T(1024)S(1)} %bitcast.90, f32[512]{0:T(512)S(1)} %bitcast.92), kind=kOutput, calls=%fused_computation.8 | convolution fusion | flops 17186160640 | bytes 46155776 | tf_op jit(solution)/shard_map/dot_general | solution.py:101
  574.8 11.7 %reshape.212 = f32[2,256,2,2048]{3,2,1,0:T(2,128)} reshape(f32[512,4096]{1,0:T(8,128)} %multiply_subtract_fusion) | data formatting | bytes 16777216 | tf_op jit(solution)/shard_map/reshape | solution.py:107
  (30 shorter events, 0.2 us)
Async XLA Ops:
  7.2 38.2 %all-gather.12.cloned.1.call-start = ((), (), s32[]{:S(2)}) async-start(), calls=%async_computation.6 | async-start | bytes 3145728 | tf_op jit(solution)/shard_map/all_gather | solution.py:39
  7.9 103.6 %all-gather.6.cloned.1.call-start = ((), (), s32[]{:S(2)}) async-start(), calls=%async_computation.1 | async-start | bytes 4456448 | tf_op jit(solution)/shard_map/all_gather | solution.py:56
  57.2 104.3 %all-gather.8.cloned.1.call-start = ((), (), s32[]{:S(2)}) async-start(), calls=%async_computation.2 | async-start | bytes 4456448 | tf_op jit(solution)/shard_map/all_gather | solution.py:57
  57.2 21.0 %copy-start.7 = (s32[4096]{0:T(1024)S(1)}, s32[4096]{0:T(1024)}, u32[]{:S(2)}) copy-start(s32[4096]{0:T(1024)} %param.13) | copy-start | bytes 49156
  57.2 22.9 %copy-start.3 = (bf16[256,2,2048]{0,2,1:T(8,128)(2,1)S(1)}, bf16[256,2,2048]{0,2,1:T(8,128)(2,1)}, u32[]{:S(2)}) copy-start(bf16[256,2,2048]{0,2,1:T(8,128)(2,1)} %copy.37) | copy-start | bytes 6291460
  89.9 7.7 %copy-start = (bf16[512,2048]{1,0:T(8,128)(2,1)S(1)}, bf16[512,2048]{1,0:T(8,128)(2,1)}, u32[]{:S(2)}) copy-start(bf16[512,2048]{1,0:T(8,128)(2,1)} %all-gather.12.cloned.1.call-done) | copy-start | bytes 6291460
  100.2 5.4 copy-start.6
  105.5 3.7 copy-start.8
  109.2 2.3 copy-start.4
  109.2 2.3 copy-start.5
  111.2 145.6 %reduce-scatter.2.cloned.1.call-start = ((), (), s32[]{:S(2)}) async-start(), calls=%async_computation.3 | async-start | bytes 6291456 | tf_op jit(solution)/shard_map/reduce_scatter | solution.py:93
  203.5 53.3 %copy-start.1 = (bf16[256,2048]{1,0:T(8,128)(2,1)S(1)}, bf16[256,2048]{1,0:T(8,128)(2,1)}, u32[]{:S(2)}) copy-start(bf16[256,2048]{1,0:T(8,128)(2,1)} %param.7) | copy-start | bytes 3145732
  203.5 225.0 %all-gather.10.cloned.1.call-start = ((), (), s32[]{:S(2)}) async-start(), calls=%async_computation.4 | async-start | bytes 35651584 | tf_op jit(solution)/shard_map/all_gather | solution.py:95
  258.7 174.8 %copy-start.2 = (bf16[256,2048]{1,0:T(8,128)(2,1)}, bf16[256,2048]{1,0:T(8,128)(2,1)S(1)}, u32[]{:S(2)}) copy-start(bf16[256,2048]{1,0:T(8,128)(2,1)S(1)} %add_convert_fusion) | copy-start | bytes 3145732
  260.4 281.2 %all-reduce.2.cloned.1.call-start = ((), (), s32[]{:S(2)}) async-start(), calls=%async_computation.5 | async-start | bytes 8388608 | tf_op jit(solution)/shard_map/psum | solution.py:13
Sparse Core Ops, SparseCore 0:
  9.5 35.8 all-gather.11
  57.3 52.4 all-gather.5
  112.5 48.8 all-gather.7
  203.7 53.0 reduce-scatter.1
  260.5 168.0 all-gather.9
  433.7 107.8 all-reduce.1
